TPU v7x, 32 devices: a whole 2x2x4 slice. The times are simulated.
32 devices in a mesh: rows: 8 (over y, x, core), experts: 4 (over z).
Axes of the slice: x: 2, y: 2, z: 4, core: 2. Of those that a mesh axis runs over, the one named last changes fastest.
Arguments:
- weight: bfloat16 [4, 8, 2048, 512], P('experts', None, 'rows'), may hold values from -3 to 3
- momentum: bfloat16 [4, 8, 2048, 512], P('experts', None, 'rows'), may hold values from -6 to 6
- gradient: bfloat16 [4, 8, 2048, 512], P('experts', None, 'rows'), may hold values from -32 to 32
- assign: int32 [4, 8], P('experts'), may hold values from 0 to 7, each once within a row
Outputs:
- new_weight: bfloat16 [4, 8, 2048, 512], P('experts', None, 'rows')
- new_momentum: bfloat16 [4, 8, 2048, 512], P('experts', None, 'rows')
Inputs may be any that keep to these rules, and one draw needn't show every extreme that they name: Each row of assign names every slot 0 to 7 exactly once; matrix i of group e keeps its momentum in slot assign[e, i].
All inputs are finite; a program needn't handle non-finite values.
Results may differ from a plain program's by a relative error of at most 0.0075.
Values may be sent and summed in bfloat16 or wider, within the bound.
A program may use at most 64 MiB of HBM per device.

v0:
```python
import math

import jax
import jax.numpy as jnp
from jax import lax
from jax.sharding import PartitionSpec as P

ROWS = 2048
COLS = 512
ITERS = 5


linear_coef = 3.4445
cubic_coef = -4.775
quintic_coef = 2.0315
beta_decay = 0.95
learn_rate = 0.5
weight_decay = 0.1
norm_epsilon = 1e-07
clip_epsilon = 1e-06


def orthogonal_stack(stack):
    widened = stack.astype(jnp.float32)
    norms = jnp.sqrt(jnp.sum(widened * widened, axis=(1, 2), keepdims=True))
    iterate = (widened / (norms + norm_epsilon)).astype(jnp.bfloat16)
    for sweep in range(ITERS):
        gram_matrix = jnp.einsum(
            "kri,krj->kij", iterate, iterate, preferred_element_type=jnp.float32
        ).astype(jnp.bfloat16)
        square = jnp.einsum(
            "kij,kjl->kil", gram_matrix, gram_matrix, preferred_element_type=jnp.float32
        )
        polynomial = (cubic_coef * gram_matrix.astype(jnp.float32) + quintic_coef * square).astype(
            jnp.bfloat16
        )
        product = jnp.einsum(
            "kri,kij->krj", iterate, polynomial, preferred_element_type=jnp.float32
        )
        iterate = (linear_coef * iterate.astype(jnp.float32) + product).astype(jnp.bfloat16)
    return iterate


def local(weight, momentum, gradient, assign):
    grad_local = gradient[0]
    mom_local = momentum[0]
    weight_local = weight[0]
    slot_table = assign[0]
    row_devices = lax.axis_size("rows")
    group_devices = lax.axis_size("experts")
    slot_count, shard_rows, col_count = grad_local.shape
    grad_wide = grad_local.astype(jnp.float32)
    sum_squares = lax.psum(jnp.sum(grad_wide * grad_wide), ("rows", "experts"))
    clip_limit = math.sqrt(float(slot_count * shard_rows * col_count * row_devices * group_devices))
    clip_factor = jnp.minimum(1.0, clip_limit / (jnp.sqrt(sum_squares) + clip_epsilon))
    inverse = jnp.argsort(slot_table)
    grad_slot = jnp.take(grad_local, inverse, axis=0)
    state = beta_decay * mom_local.astype(jnp.float32) + clip_factor * grad_slot.astype(jnp.float32)
    owned_count = slot_count // row_devices
    update = (clip_factor * grad_slot.astype(jnp.float32) + beta_decay * state).astype(jnp.bfloat16)
    received = lax.all_to_all(
        update.reshape(row_devices, owned_count, shard_rows, col_count),
        "rows",
        split_axis=0,
        concat_axis=2,
        tiled=True,
    )
    count = received.shape[1]
    stacked = received.reshape(count, received.shape[2], col_count)
    result = orthogonal_stack(stacked).reshape(received.shape)
    returned = lax.all_to_all(result, "rows", split_axis=2, concat_axis=0, tiled=True)
    ortho_slot = returned.reshape(slot_count, shard_rows, col_count)
    ortho = jnp.take(ortho_slot, slot_table, axis=0)
    shape_scale = 0.2 * math.sqrt(max(ROWS, COLS))
    new_weight = weight_local.astype(jnp.float32) * (
        1.0 - learn_rate * weight_decay
    ) - learn_rate * shape_scale * ortho.astype(jnp.float32)
    return (new_weight.astype(jnp.bfloat16)[None], state.astype(jnp.bfloat16)[None])


def solution(mesh):
    placed = (
        P("experts", None, "rows", None),
        P("experts", None, "rows", None),
        P("experts", None, "rows", None),
        P("experts", None),
    )
    return jax.shard_map(
        local,
        mesh=mesh,
        in_specs=placed,
        out_specs=(P("experts", None, "rows", None), P("experts", None, "rows", None)),
        check_vma=False,
    )
```

profile of v0, /device:TPU:0, one launch (start us, length us, event | category | flops | bytes accessed | tf_op | source)
XLA Modules:
  0.0 187.8 jit_solution(6475272698746676409)
XLA Ops:
  0.6 1.6 sort.17
  2.3 3.3 %multiply_reduce_fusion = f32[]{:T(128)} fusion(bf16[1,8,256,512]{3,2,1,0:T(8,128)(2,1)} %param.8), kind=kLoop, calls=%fused_computation.17 | loop fusion | flops 3145727 | bytes 2097156 | tf_op jit(solution)/shard_map/reduce_sum | solution.py:53
  5.5 42.2 %psum.7 = f32[]{:T(128)} all-reduce(f32[]{:T(128)} %multiply_reduce_fusion), channel_id=1, replica_groups=mesh['rows'=8,'experts'=4] {'rows','experts'}, use_global_device_ids=true, to_apply=%region_1.0 | all-reduce | flops 1 | bytes 8 | tf_op jit(solution)/shard_map/psum | solution.py:53
  48.4 2.3 %gather_fusion = bf16[8,256,512]{2,1,0:T(8,128)(2,1)S(1)} fusion(bf16[8,256,512]{2,1,0:T(8,128)(2,1)} %bitcast.78, s32[1024]{0:T(1024)S(1)} %pad_clamp_fusion.1), kind=kCustom, calls=%fused_computation.clone | custom fusion | bytes 4194336 | tf_op jit(solution)/shard_map/jit(_take)/gather | solution.py:57
  50.7 4.2 %fusion.5 = (bf16[1,8,256,512]{3,2,1,0:T(8,128)(2,1)}, bf16[8,1,256,512]{3,2,1,0:T(8,128)(2,1)S(1)}) fusion(bf16[1,8,256,512]{3,2,1,0:T(8,128)(2,1)} %param.7, f32[]{:T(128)S(6)} %min_shard_map.3, bf16[8,256,512]{2,1,0:T(8,128)(2,1)S(1)} %gather_fusion, pred[8]{0:T(512)(128)(4,1)S(1)} %compare_and_fusion.1), kind=kLoop, calls=%fused_computation.19 | loop fusion | flops 10485760 | bytes 8388620 | tf_op jit(solution)/shard_map/broadcast_in_dim | solution.py:78
  54.9 30.1 %all_to_all.8 = bf16[8,1,256,512]{3,2,1,0:T(8,128)(2,1)S(1)} all-to-all(bf16[8,1,256,512]{3,2,1,0:T(8,128)(2,1)S(1)} %get-tuple-element.6), channel_id=1, replica_groups=mesh['rows'=8,'experts'=4] {'rows'}, dimensions={0} | all-to-all | bytes 4194304 | tf_op jit(solution)/shard_map/all_to_all | solution.py:61
  85.0 1.7 fusion
  87.4 0.4 fusion.1
  87.8 0.0 copy-start.3
  87.8 1.3 fusion.23
  89.1 0.0 copy-done.3
  89.1 3.8 %add_convert_fusion.4 = bf16[2048,512]{1,0:T(8,128)(2,1)S(1)} fusion(bf16[2048,512]{1,0:T(8,128)(2,1)} %bitcast.79, bf16[512,512]{1,0:T(8,128)(2,1)S(1)} %fusion.23), kind=kOutput, calls=%fused_computation.13 | convolution fusion | flops 1347682304 | bytes 4718592 | tf_op jit(solution)/shard_map/kri,kij->krj/dot_general | solution.py:37
  93.0 1.3 convolution_convert_fusion.3
  94.2 2.9 %add_convert_fusion.3 = bf16[2048,512]{1,0:T(8,128)(2,1)} fusion(bf16[2048,512]{1,0:T(8,128)(2,1)S(1)} %add_convert_fusion.4, bf16[512,512]{1,0:T(8,128)(2,1)S(1)} %convolution_convert_fusion.3), kind=kOutput, calls=%fused_computation.12 | convolution fusion | flops 1347682304 | bytes 4718592 | tf_op jit(solution)/shard_map/kri,kij->krj/dot_general | solution.py:37
  97.2 0.0 copy-start
  97.2 3.6 %convolution_convert_fusion.2 = bf16[512,512]{1,0:T(8,128)(2,1)S(1)} fusion(bf16[2048,512]{1,0:T(8,128)(2,1)} %add_convert_fusion.3), kind=kOutput, calls=%fused_computation.44 | convolution fusion | flops 1074003968 | bytes 2621440 | tf_op jit(solution)/shard_map/kri,krj->kij/dot_general | solution.py:28
  100.8 0.0 copy-done
  100.8 2.9 %add_convert_fusion.2 = bf16[2048,512]{1,0:T(8,128)(2,1)} fusion(bf16[2048,512]{1,0:T(8,128)(2,1)S(1)} %copy-done, bf16[512,512]{1,0:T(8,128)(2,1)S(1)} %convolution_convert_fusion.2), kind=kOutput, calls=%fused_computation.11 | convolution fusion | flops 1347682304 | bytes 4718592 | tf_op jit(solution)/shard_map/kri,kij->krj/dot_general | solution.py:37
  103.8 0.0 copy-start.1
  103.8 3.6 %convolution_convert_fusion.1 = bf16[512,512]{1,0:T(8,128)(2,1)S(1)} fusion(bf16[2048,512]{1,0:T(8,128)(2,1)} %add_convert_fusion.2), kind=kOutput, calls=%fused_computation.43 | convolution fusion | flops 1074003968 | bytes 2621440 | tf_op jit(solution)/shard_map/kri,krj->kij/dot_general | solution.py:28
  107.4 0.0 copy-done.1
  107.5 2.9 %add_convert_fusion.1 = bf16[2048,512]{1,0:T(8,128)(2,1)} fusion(bf16[2048,512]{1,0:T(8,128)(2,1)S(1)} %copy-done.1, bf16[512,512]{1,0:T(8,128)(2,1)S(1)} %convolution_convert_fusion.1), kind=kOutput, calls=%fused_computation.10 | convolution fusion | flops 1347682304 | bytes 4718592 | tf_op jit(solution)/shard_map/kri,kij->krj/dot_general | solution.py:37
  110.4 0.0 copy-start.2
  110.4 3.6 %convolution_convert_fusion = bf16[512,512]{1,0:T(8,128)(2,1)S(1)} fusion(bf16[2048,512]{1,0:T(8,128)(2,1)} %add_convert_fusion.1), kind=kOutput, calls=%fused_computation.42 | convolution fusion | flops 1074003968 | bytes 2621440 | tf_op jit(solution)/shard_map/kri,krj->kij/dot_general | solution.py:28
  114.0 0.0 copy-done.2
  114.1 2.9 %fusion.4 = bf16[1,1,2048,512]{3,2,1,0:T(8,128)(2,1)} fusion(bf16[2048,512]{1,0:T(8,128)(2,1)S(1)} %copy-done.2, bf16[512,512]{1,0:T(8,128)(2,1)S(1)} %convolution_convert_fusion), kind=kOutput, calls=%fused_computation.18 | convolution fusion | flops 1347682304 | bytes 4718592 | tf_op jit(solution)/shard_map/kri,kij->krj/dot_general | solution.py:37
  117.0 7.5 %copy.17 = bf16[1,1,2048,512]{3,1,0,2:T(2,128)(2,1)} copy(bf16[1,1,2048,512]{3,2,1,0:T(8,128)(2,1)} %fusion.4) | data formatting | bytes 4194304 | tf_op jit(solution)/shard_map/reshape | solution.py:70
  124.5 0.5 broadcast.149
  125.0 14.1 %reduce.2 = bf16[2048,512]{1,0:T(8,128)(2,1)S(1)} reduce(bf16[2048,1,1,512]{3,2,1,0:T(2,128)(2,1)} %bitcast.75, bf16[]{:T(256)} %broadcast.149), dimensions={1,2}, to_apply=%bitcast.74.reduce_sub_computation | reduce | bytes 4194306
  139.1 3.8 %reshape.220 = bf16[8,2,65536]{2,1,0:T(2,128)(2,1)} reshape(bf16[2048,512]{1,0:T(8,128)(2,1)S(1)} %reduce.2) | data formatting | bytes 4194304
  142.8 0.0 copy-start.4
  142.8 3.7 %all-to-all-start.1 = ((bf16[8,2,65536]{2,1,0:T(2,128)(2,1)}), bf16[8,2,65536]{2,1,0:T(2,128)(2,1)S(1)}, u32[]{:S(2)}, u32[]{:S(2)}) async-start(bf16[8,2,65536]{2,1,0:T(2,128)(2,1)} %reshape.220), calls=%async_computation.1 | async-start | bytes 4194304 | tf_op jit(solution)/shard_map/all_to_all | solution.py:71
  146.6 0.0 copy-done.4
  146.6 26.5 %all-to-all-done.1 = bf16[8,2,65536]{2,1,0:T(2,128)(2,1)S(1)} async-done(((bf16[8,2,65536]{2,1,0:T(2,128)(2,1)}), bf16[8,2,65536]{2,1,0:T(2,128)(2,1)S(1)}, u32[]{:S(2)}, u32[]{:S(2)}) %all-to-all-start.1) | async-done | bytes 2097184 | tf_op jit(solution)/shard_map/all_to_all | solution.py:71
  173.1 4.4 %reshape.221 = bf16[2048,1,1,512]{3,2,1,0:T(2,128)(2,1)} reshape(bf16[8,2,65536]{2,1,0:T(2,128)(2,1)S(1)} %all-to-all-done.1) | data formatting | bytes 4194304
  177.5 4.1 %copy.15 = bf16[1,1,2048,512]{3,2,0,1:T(8,128)(2,1)} copy(bf16[1,1,2048,512]{3,1,0,2:T(2,128)(2,1)} %bitcast.76) | data formatting | bytes 4194304
  181.6 2.3 %gather_fusion.1 = bf16[8,256,512]{2,1,0:T(8,128)(2,1)S(1)} fusion(bf16[8,256,512]{2,1,0:T(8,128)(2,1)} %bitcast.77, s32[1024]{0:T(1024)S(1)} %pad_clamp_fusion), kind=kCustom, calls=%fused_computation.1.clone | custom fusion | bytes 4194336 | tf_op jit(solution)/shard_map/jit(_take)/gather | solution.py:73
  183.9 3.9 %fusion.7 = bf16[1,8,256,512]{3,2,1,0:T(8,128)(2,1)} fusion(bf16[1,8,256,512]{3,2,1,0:T(8,128)(2,1)} %param.6, bf16[8,256,512]{2,1,0:T(8,128)(2,1)S(1)} %gather_fusion.1, pred[8]{0:T(512)(128)(4,1)S(1)} %compare_and_fusion), kind=kLoop, calls=%fused_computation.21 | loop fusion | flops 7340032 | bytes 6291464 | tf_op jit(solution)/shard_map/broadcast_in_dim | solution.py:78
  (7 shorter events, 0.0 us)
Async XLA Ops:
  87.8 1.3 copy-start.3
  97.2 3.6 %copy-start = (bf16[2048,512]{1,0:T(8,128)(2,1)S(1)}, bf16[2048,512]{1,0:T(8,128)(2,1)}, u32[]{:S(2)}) copy-start(bf16[2048,512]{1,0:T(8,128)(2,1)} %add_convert_fusion.3) | copy-start | bytes 6291460
  103.8 3.7 %copy-start.1 = (bf16[2048,512]{1,0:T(8,128)(2,1)S(1)}, bf16[2048,512]{1,0:T(8,128)(2,1)}, u32[]{:S(2)}) copy-start(bf16[2048,512]{1,0:T(8,128)(2,1)} %add_convert_fusion.2) | copy-start | bytes 6291460
  110.4 3.6 %copy-start.2 = (bf16[2048,512]{1,0:T(8,128)(2,1)S(1)}, bf16[2048,512]{1,0:T(8,128)(2,1)}, u32[]{:S(2)}) copy-start(bf16[2048,512]{1,0:T(8,128)(2,1)} %add_convert_fusion.1) | copy-start | bytes 6291460
  142.8 3.7 %copy-start.4 = (s32[1,8]{1,0:T(1,128)S(1)}, s32[1,8]{1,0:T(1,128)}, u32[]{:S(2)}) copy-start(s32[1,8]{1,0:T(1,128)} %param.9) | copy-start | bytes 100
  142.8 30.3 %all-to-all-start.1 = ((bf16[8,2,65536]{2,1,0:T(2,128)(2,1)}), bf16[8,2,65536]{2,1,0:T(2,128)(2,1)S(1)}, u32[]{:S(2)}, u32[]{:S(2)}) async-start(bf16[8,2,65536]{2,1,0:T(2,128)(2,1)} %reshape.220), calls=%async_computation.1 | async-start | bytes 4194304 | tf_op jit(solution)/shard_map/all_to_all | solution.py:71
where the time goes:
time: 188 us
  blocking collectives  72.3 us (38%)
  other arithmetic  29.1 us (15%)
  matrix products  29.1 us (15%)
  waiting for transfers between devices  26.5 us (14%)
  local copies, waits for them, and re-layouts  24.8 us (13%)
  starting transfers between devices  3.74 us (2%)
  between operations  2.22 us (1%)
    psum x1, blocking collectives, local(): sum_squares = lax.psum(jnp.sum(grad_wide * grad_wide), ('rows', 'experts'))  42.2 us
    all_to_all x1, blocking collectives, local(): lax.all_to_all(update.reshape(row_devices, owned_count, shard_rows, col_c...  30.1 us
    all_to_all x1, waiting for transfers between devices, local(): lax.all_to_all(result, 'rows', split_axis=2, concat_axis=0, tiled=True)  26.5 us
    dot_general x5, matrix products, orthogonal_stack(): jnp.einsum('kri,kij->krj', iterate, polynomial, preferred_element_type=jn...  15.6 us
    unnamed x1, other arithmetic  14.1 us
    dot_general x5, matrix products, orthogonal_stack(): jnp.einsum('kri,krj->kij', iterate, iterate, preferred_element_type=jnp.f...  13.5 us
    unnamed x14, local copies, waits for them, and re-layouts  12.8 us
    reshape x1, local copies, waits for them, and re-layouts, local(): result = orthogonal_stack(stacked).reshape(received.shape)  7.46 us
  transfers between devices with their start and end apart: 1, of which 1 were waited for; matrix products, arithmetic and copies ran while one was open for 0% of the time, Pallas kernels for 0%

commit v1 on v0

v1 whole, which is shorter than its diff:
```python
import functools
import math

import jax
import jax.numpy as jnp
from jax import lax
from jax.experimental import pallas as pl
from jax.experimental.pallas import tpu as pltpu
from jax.sharding import PartitionSpec as P

ITERS = 5
linear_coef = 3.4445
cubic_coef = -4.775
quintic_coef = 2.0315
beta_decay = 0.95
learn_rate = 0.5
weight_decay = 0.1
norm_epsilon = 1e-07
clip_epsilon = 1e-06
MESH = pl.DeviceIdType.MESH
F32 = jnp.float32
BF16 = jnp.bfloat16


def gram_of(block):
    return lax.dot_general(block, block, (((0,), (0,)), ((), ())), preferred_element_type=F32)


def polynomial(gram):
    rounded = gram.astype(BF16)
    square = jnp.dot(rounded, rounded, preferred_element_type=F32)
    return (cubic_coef * rounded.astype(F32) + quintic_coef * square).astype(BF16)


def kernel(
    n, groups, block_rows,
    assign, w_hbm, m_hbm, g_hbm,
    nw_ref, nm_ref,
    w_v, m_v, g_v, out_v, mom_v, send_v, recv_v, back_v, x_v, gram_v, poly_v, row_part, group_part,
    load_sem, store_sem, rs_send, rs_recv, gs_send, gs_recv, f_send, f_recv, b_send, b_recv,
):
    me = lax.axis_index("rows")
    group = lax.axis_index("experts")
    slots, shard_rows, cols = g_v.shape

    barrier = pltpu.get_barrier_semaphore()

    def greet_row(k, carry):
        pl.semaphore_signal(barrier, inc=1, device_id={"rows": lax.rem(me + k, n)}, device_id_type=MESH)
        return carry

    def greet_group(k, carry):
        pl.semaphore_signal(
            barrier, inc=1, device_id={"experts": lax.rem(group + k, groups)}, device_id_type=MESH
        )
        return carry

    lax.fori_loop(1, n, greet_row, 0)
    lax.fori_loop(1, groups, greet_group, 0)
    load_g = pltpu.make_async_copy(g_hbm, g_v, load_sem.at[0])
    load_m = pltpu.make_async_copy(m_hbm, m_v, load_sem.at[1])
    load_w = pltpu.make_async_copy(w_hbm, w_v, load_sem.at[2])
    load_g.start()
    load_m.start()
    load_w.start()
    load_g.wait()

    def square_sum(i, total):
        wide = g_v[i].astype(F32)
        return total + jnp.sum((wide * wide).reshape(shard_rows // 8, 8, cols), axis=0)

    partial = lax.fori_loop(0, slots, square_sum, jnp.zeros((8, cols), F32))
    tile = partial[:, :128]
    for c in range(1, cols // 128):
        tile = tile + partial[:, c * 128 : (c + 1) * 128]
    row_part[me] = tile
    pl.semaphore_wait(barrier, n + groups - 2)

    def row_sum_copy(k, source):
        return pltpu.make_async_remote_copy(
            src_ref=row_part.at[me],
            dst_ref=row_part.at[source],
            send_sem=rs_send.at[k],
            recv_sem=rs_recv.at[source],
            device_id={"rows": lax.rem(me + k, n)},
            device_id_type=MESH,
        )

    def start_row(k, carry):
        row_sum_copy(k, me).start()
        return carry

    def wait_row(k, carry):
        row_sum_copy(k, lax.rem(me + k, n)).wait_recv()
        return carry

    def drain_row(k, carry):
        row_sum_copy(k, me).wait_send()
        return carry

    lax.fori_loop(1, n, start_row, 0)
    lax.fori_loop(1, n, wait_row, 0)
    group_part[group] = jnp.sum(row_part[...], axis=0)

    def group_sum_copy(k, source):
        return pltpu.make_async_remote_copy(
            src_ref=group_part.at[group],
            dst_ref=group_part.at[source],
            send_sem=gs_send.at[k],
            recv_sem=gs_recv.at[source],
            device_id={"experts": lax.rem(group + k, groups)},
            device_id_type=MESH,
        )

    def start_group(k, carry):
        group_sum_copy(k, group).start()
        return carry

    def wait_group(k, carry):
        group_sum_copy(k, lax.rem(group + k, groups)).wait_recv()
        return carry

    def drain_group(k, carry):
        group_sum_copy(k, group).wait_send()
        return carry

    lax.fori_loop(1, groups, start_group, 0)
    load_m.wait()
    lax.fori_loop(1, groups, wait_group, 0)
    sum_squares = jnp.sum(jnp.sum(group_part[...], axis=0), axis=(0, 1), keepdims=True)
    clip_limit = math.sqrt(float(slots * shard_rows * cols * n * groups))
    clip = jnp.minimum(1.0, clip_limit / (jnp.sqrt(sum_squares) + clip_epsilon))

    def forward_copy(target, source):
        return pltpu.make_async_remote_copy(
            src_ref=send_v.at[target],
            dst_ref=recv_v.at[source],
            send_sem=f_send.at[target],
            recv_sem=f_recv.at[source],
            device_id={"rows": target},
            device_id_type=MESH,
        )

    def update_of(i):
        scaled = clip * g_v[i].astype(F32)
        state = beta_decay * m_v[assign[0, i]].astype(F32) + scaled
        return (scaled + beta_decay * state).astype(BF16)

    def send_update(k, carry):
        target = lax.rem(me + k, n)
        send_v[target] = update_of(target)
        forward_copy(target, me).start()
        return carry

    lax.fori_loop(1, n, send_update, 0)
    own = update_of(me)
    recv_v[me] = own
    gram_v[...] = gram_of(own)

    def momentum_of(p, carry):
        index = lax.fori_loop(
            0, slots, lambda i, found: jnp.where(assign[0, i] == p, i, found), jnp.int32(0)
        )
        mom_v[p] = (
            beta_decay * m_v[p].astype(F32) + clip * g_v[index].astype(F32)
        ).astype(BF16)
        return carry

    lax.fori_loop(0, slots, momentum_of, 0)
    store_m = pltpu.make_async_copy(mom_v, nm_ref, store_sem.at[0])
    store_m.start()

    def take_update(k, carry):
        source = lax.rem(me + k, n)
        forward_copy(source, source).wait_recv()
        gram_v[...] += gram_of(recv_v[source])
        return carry

    lax.fori_loop(1, n, take_update, 0)

    gram = gram_v[...]
    diagonal = lax.broadcasted_iota(jnp.int32, gram.shape, 0) == lax.broadcasted_iota(
        jnp.int32, gram.shape, 1
    )
    trace = jnp.sum(jnp.where(diagonal, gram, 0.0), axis=(0, 1), keepdims=True)
    scale = 1.0 / (jnp.sqrt(trace) + norm_epsilon)
    poly_v[...] = polynomial(gram * scale * scale)

    shards = block_rows // shard_rows
    for b in range(n // shards):
        x = recv_v[pl.ds(b * shards, shards)].reshape(block_rows, cols)
        product = jnp.dot(x, poly_v[...], preferred_element_type=F32)
        x = (scale * (linear_coef * x.astype(F32) + product)).astype(BF16)
        x_v[pl.ds(b * block_rows, block_rows)] = x
        if b == 0:
            gram_v[...] = gram_of(x)
        else:
            gram_v[...] += gram_of(x)

    def sweep(t, carry):
        poly_v[...] = polynomial(gram_v[...])
        for b in range(n // shards):
            rows = pl.ds(b * block_rows, block_rows)
            x = x_v[rows]
            product = jnp.dot(x, poly_v[...], preferred_element_type=F32)
            x = (linear_coef * x.astype(F32) + product).astype(BF16)
            x_v[rows] = x
            if b == 0:
                gram_v[...] = gram_of(x)
            else:
                gram_v[...] += gram_of(x)
        return carry

    lax.fori_loop(1, ITERS - 1, sweep, 0)
    poly_v[...] = polynomial(gram_v[...])

    def last_rows(i):
        x = x_v[pl.ds(pl.multiple_of(i * shard_rows, shard_rows), shard_rows)]
        product = jnp.dot(x, poly_v[...], preferred_element_type=F32)
        return (linear_coef * x.astype(F32) + product).astype(BF16)

    def back_copy(target, source):
        return pltpu.make_async_remote_copy(
            src_ref=send_v.at[target],
            dst_ref=back_v.at[source],
            send_sem=b_send.at[target],
            recv_sem=b_recv.at[source],
            device_id={"rows": target},
            device_id_type=MESH,
        )

    def send_back(k, carry):
        target = lax.rem(me + k, n)
        forward_copy(target, me).wait_send()
        send_v[target] = last_rows(target)
        back_copy(target, me).start()
        return carry

    lax.fori_loop(1, n, send_back, 0)
    step = learn_rate * 0.2 * math.sqrt(max(n * shard_rows, cols))
    load_w.wait()

    def weight_of(i, ortho):
        out_v[i] = (
            w_v[i].astype(F32) * (1.0 - learn_rate * weight_decay) - step * ortho.astype(F32)
        ).astype(BF16)
        pltpu.make_async_copy(out_v.at[i], nw_ref.at[i], f_send.at[i]).start()

    weight_of(me, last_rows(me))

    def take_back(k, carry):
        source = lax.rem(me + k, n)
        back_copy(source, source).wait_recv()
        weight_of(source, back_v[source])
        return carry

    lax.fori_loop(1, n, take_back, 0)
    lax.fori_loop(1, n, drain_row, 0)
    lax.fori_loop(1, groups, drain_group, 0)

    def drain_back(k, carry):
        back_copy(lax.rem(me + k, n), me).wait_send()
        return carry

    lax.fori_loop(1, n, drain_back, 0)

    def drain_out(i, carry):
        pltpu.make_async_copy(out_v.at[i], nw_ref.at[i], f_send.at[i]).wait()
        return carry

    lax.fori_loop(0, n, drain_out, 0)
    store_m.wait()


def local(weight, momentum, gradient, assign):
    n = lax.axis_size("rows")
    groups = lax.axis_size("experts")
    _, slots, shard_rows, cols = gradient.shape
    assert slots == n
    block_rows = min(1024, n * shard_rows)
    shape = (slots, shard_rows, cols)
    new_weight, new_momentum = pl.pallas_call(
        functools.partial(kernel, n, groups, block_rows),
        out_shape=(jax.ShapeDtypeStruct(shape, BF16),) * 2,
        in_specs=[pl.BlockSpec(memory_space=pltpu.SMEM)] + [pl.BlockSpec(memory_space=pl.ANY)] * 3,
        out_specs=(pl.BlockSpec(memory_space=pl.ANY),) * 2,
        scratch_shapes=[pltpu.VMEM(shape, BF16)] * 8
        + [
            pltpu.VMEM((n * shard_rows, cols), BF16),
            pltpu.VMEM((cols, cols), F32),
            pltpu.VMEM((cols, cols), BF16),
            pltpu.VMEM((n, 8, 128), F32),
            pltpu.VMEM((groups, 8, 128), F32),
            pltpu.SemaphoreType.DMA((3,)),
            pltpu.SemaphoreType.DMA((1,)),
            pltpu.SemaphoreType.DMA((n,)),
            pltpu.SemaphoreType.DMA((n,)),
            pltpu.SemaphoreType.DMA((groups,)),
            pltpu.SemaphoreType.DMA((groups,)),
            pltpu.SemaphoreType.DMA((n,)),
            pltpu.SemaphoreType.DMA((n,)),
            pltpu.SemaphoreType.DMA((n,)),
            pltpu.SemaphoreType.DMA((n,)),
        ],
        compiler_params=pltpu.CompilerParams(
            collective_id=0, has_side_effects=True, vmem_limit_bytes=48 << 20
        ),
        name="muon_step",
    )(assign, weight[0], momentum[0], gradient[0])
    return new_weight[None], new_momentum[None]


def solution(mesh):
    placed = P("experts", None, "rows", None)
    return jax.shard_map(
        local,
        mesh=mesh,
        in_specs=(placed, placed, placed, P("experts", None)),
        out_specs=(placed, placed),
        check_vma=False,
    )
```

time: 188 us -> 77.3 us (0.41)
  the two profiles are of different devices: /device:TPU:0 before, /device:TPU:1 now
where the time goes in v1:
time: 77.3 us; the launch traced here: 77.2 us
  Pallas kernels  73.2 us (95%)
  local copies, waits for them, and re-layouts  3.29 us (4%)
    pallas_call x1, Pallas kernels, local(): pl.pallas_call(functools.partial(kernel, n, groups, block_rows), out_shap...  73.2 us
    unnamed x4, local copies, waits for them, and re-layouts  3.29 us

profile of v1, /device:TPU:1, one launch (start us, length us, event | category | flops | bytes accessed | tf_op | source)
XLA Modules:
  0.0 77.2 jit_solution(16347573274527424291)
XLA Ops:
  0.6 0.0 copy-start
  0.6 0.6 copy-done
  1.3 73.2 %muon_step.1 = (bf16[8,256,512]{2,1,0:T(8,128)(2,1)S(1)}, bf16[8,256,512]{2,1,0:T(8,128)(2,1)S(1)}) custom-call(s32[1,8]{1,0:T(1,128)S(1)} %copy-done, bf16[8,256,512]{2,1,0:T(8,128)(2,1)} %bitcast.7, bf16[8,256,512]{2,1,0:T(8,128)(2,1)} %bitcast.8, bf16[8,256,512]{2,1,0:T(8,128)(2,1)} %bitcast.9), custom_call_target="tpu_custom_call" | custom-call | tf_op jit(solution)/shard_map/muon_step/pallas_call | solution.py:282
  74.5 1.3 %copy.8 = bf16[1,8,256,512]{3,2,1,0:T(8,128)(2,1)} copy(bf16[1,8,256,512]{3,2,1,0:T(8,128)(2,1)S(1)} %bitcast.6) | data formatting | bytes 4194304
  75.9 1.3 %copy.9 = bf16[1,8,256,512]{3,2,1,0:T(8,128)(2,1)} copy(bf16[1,8,256,512]{3,2,1,0:T(8,128)(2,1)S(1)} %bitcast.5) | data formatting | bytes 4194304
Async XLA Ops:
  0.6 0.7 copy-start

commit v2 on v1

v2 whole, which is shorter than its diff:
```python
import functools
import math

import jax
import jax.numpy as jnp
from jax import lax
from jax.experimental import pallas as pl
from jax.experimental.pallas import tpu as pltpu
from jax.sharding import PartitionSpec as P

ITERS = 5
first_steps = 3
linear_coef = 3.4445
cubic_coef = -4.775
quintic_coef = 2.0315
beta_decay = 0.95
learn_rate = 0.5
weight_decay = 0.1
norm_epsilon = 1e-07
clip_epsilon = 1e-06
MESH = pl.DeviceIdType.MESH
F32 = jnp.float32
BF16 = jnp.bfloat16


def gram_of(block):
    return lax.dot_general(block, block, (((0,), (0,)), ((), ())), preferred_element_type=F32)


def dot(a, b):
    return jnp.dot(a, b, preferred_element_type=F32)


def factor(gram):
    rows = lax.broadcasted_iota(jnp.int32, gram.shape, 0)
    columns = lax.broadcasted_iota(jnp.int32, gram.shape, 1)
    wide = cubic_coef * gram.astype(F32) + quintic_coef * dot(gram, gram)
    return jnp.where(rows == columns, wide + linear_coef, wide).astype(BF16)


def chain(steps, split, gram_v, poly_v):
    for t in range(steps):
        gram = gram_v[...]
        high = gram.astype(BF16)
        q = factor(high)
        if t < steps - 1:
            half = dot(high, q)
            if split:
                half += dot((gram - high.astype(F32)).astype(BF16), q)
            gram_v[...] = dot(half.astype(BF16), q)
        poly_v[...] = q if t == 0 else dot(poly_v[...], q).astype(BF16)


def kernel(
    n, groups, block_rows,
    assign, w_hbm, m_hbm, g_hbm,
    nw_ref, nm_ref,
    w_v, m_v, g_v, send_v, recv_v, back_v, x_v, gram_v, poly_v, part,
    load_sem, s_send, s_recv, f_send, f_recv, b_send, b_recv,
):
    me = lax.axis_index("rows")
    group = lax.axis_index("experts")
    slots, shard_rows, cols = g_v.shape

    barrier = pltpu.get_barrier_semaphore()

    devices = n * groups
    here = group * n + me

    def device(k):
        index = lax.rem(here + k, devices)
        return index, {"experts": index // n, "rows": lax.rem(index, n)}

    def greet(k, carry):
        pl.semaphore_signal(barrier, inc=1, device_id=device(k)[1], device_id_type=MESH)
        return carry

    lax.fori_loop(1, devices, greet, 0)
    load_g = pltpu.make_async_copy(g_hbm, g_v, load_sem.at[0])
    load_m = pltpu.make_async_copy(m_hbm, m_v, load_sem.at[1])
    load_w = pltpu.make_async_copy(w_hbm, w_v, load_sem.at[2])
    load_g.start()
    load_m.start()
    load_w.start()
    load_g.wait()

    def square_sum(i, total):
        wide = g_v[i].astype(F32)
        return total + jnp.sum((wide * wide).reshape(shard_rows // 8, 8, cols), axis=0)

    partial = lax.fori_loop(0, slots, square_sum, jnp.zeros((8, cols), F32))
    tile = partial[:, :128]
    for c in range(1, cols // 128):
        tile = tile + partial[:, c * 128 : (c + 1) * 128]
    part[here] = tile
    pl.semaphore_wait(barrier, devices - 1)

    def sum_copy(k, source):
        return pltpu.make_async_remote_copy(
            src_ref=part.at[here],
            dst_ref=part.at[source],
            send_sem=s_send.at[k],
            recv_sem=s_recv.at[source],
            device_id=device(k)[1],
            device_id_type=MESH,
        )

    def start_sum(k, carry):
        sum_copy(k, here).start()
        return carry

    def wait_sum(k, carry):
        sum_copy(k, device(k)[0]).wait_recv()
        return carry

    def drain_sum(k, carry):
        sum_copy(k, here).wait_send()
        return carry

    lax.fori_loop(1, devices, start_sum, 0)
    load_m.wait()
    lax.fori_loop(1, devices, wait_sum, 0)
    sum_squares = jnp.sum(jnp.sum(part[...], axis=0), axis=(0, 1), keepdims=True)
    clip_limit = math.sqrt(float(slots * shard_rows * cols * n * groups))
    clip = jnp.minimum(1.0, clip_limit / (jnp.sqrt(sum_squares) + clip_epsilon))

    def forward_copy(target, source):
        return pltpu.make_async_remote_copy(
            src_ref=send_v.at[target],
            dst_ref=recv_v.at[source],
            send_sem=f_send.at[target],
            recv_sem=f_recv.at[source],
            device_id={"rows": target},
            device_id_type=MESH,
        )

    def update_of(i):
        scaled = clip * g_v[i].astype(F32)
        state = beta_decay * m_v[assign[0, i]].astype(F32) + scaled
        return (scaled + beta_decay * state).astype(BF16)

    def peer(k):
        return lax.rem(me + 1 + lax.rem(k, n - 1), n)

    def send_update(k, carry):
        target = peer(k)
        send_v[target] = update_of(target)
        forward_copy(target, me).start()
        return carry

    lax.fori_loop(1, n, send_update, 0)
    own = update_of(me)
    recv_v[me] = own
    gram_v[...] = gram_of(own)

    def momentum_of(p, carry):
        index = lax.fori_loop(
            0, slots, lambda i, found: jnp.where(assign[0, i] == p, i, found), jnp.int32(0)
        )
        nm_ref[p] = (
            beta_decay * m_v[p].astype(F32) + clip * g_v[index].astype(F32)
        ).astype(BF16)
        return carry

    lax.fori_loop(0, slots, momentum_of, 0)

    def take_update(k, carry):
        source = lax.rem(me + n - 1 - lax.rem(k, n - 1), n)
        forward_copy(source, source).wait_recv()
        gram_v[...] += gram_of(recv_v[source])
        return carry

    lax.fori_loop(1, n, take_update, 0)

    gram = gram_v[...]
    diagonal = lax.broadcasted_iota(jnp.int32, gram.shape, 0) == lax.broadcasted_iota(
        jnp.int32, gram.shape, 1
    )
    trace = jnp.sum(jnp.where(diagonal, gram, 0.0), axis=(0, 1), keepdims=True)
    scale = 1.0 / (jnp.sqrt(trace) + norm_epsilon)
    gram_v[...] = gram * (scale * scale)
    chain(first_steps, True, gram_v, poly_v)

    shards = block_rows // shard_rows
    for b in range(n // shards):
        x = recv_v[pl.ds(b * shards, shards)].reshape(block_rows, cols)
        x = (scale * dot(x, poly_v[...])).astype(BF16)
        x_v[pl.ds(b * block_rows, block_rows)] = x
        if b == 0:
            gram_v[...] = gram_of(x)
        else:
            gram_v[...] += gram_of(x)

    chain(ITERS - first_steps, False, gram_v, poly_v)

    def last_rows(i):
        x = x_v[pl.ds(pl.multiple_of(i * shard_rows, shard_rows), shard_rows)]
        return dot(x, poly_v[...]).astype(BF16)

    def back_copy(target, source):
        return pltpu.make_async_remote_copy(
            src_ref=send_v.at[target],
            dst_ref=back_v.at[source],
            send_sem=b_send.at[target],
            recv_sem=b_recv.at[source],
            device_id={"rows": target},
            device_id_type=MESH,
        )

    def send_back(k, carry):
        target = peer(k)
        forward_copy(target, me).wait_send()
        send_v[target] = last_rows(target)
        back_copy(target, me).start()
        return carry

    lax.fori_loop(1, n, send_back, 0)
    step = learn_rate * 0.2 * math.sqrt(max(n * shard_rows, cols))
    load_w.wait()

    def weight_of(i, ortho):
        nw_ref[i] = (
            w_v[i].astype(F32) * (1.0 - learn_rate * weight_decay) - step * ortho.astype(F32)
        ).astype(BF16)

    weight_of(me, last_rows(me))

    def take_back(k, carry):
        source = lax.rem(me + n - 1 - lax.rem(k, n - 1), n)
        back_copy(source, source).wait_recv()
        weight_of(source, back_v[source])
        return carry

    lax.fori_loop(1, n, take_back, 0)
    lax.fori_loop(1, devices, drain_sum, 0)

    def drain_back(k, carry):
        back_copy(lax.rem(me + k, n), me).wait_send()
        return carry

    lax.fori_loop(1, n, drain_back, 0)


def local(weight, momentum, gradient, assign):
    n = lax.axis_size("rows")
    groups = lax.axis_size("experts")
    _, slots, shard_rows, cols = gradient.shape
    assert slots == n
    block_rows = min(1024, n * shard_rows)
    shape = (slots, shard_rows, cols)
    new_weight, new_momentum = pl.pallas_call(
        functools.partial(kernel, n, groups, block_rows),
        out_shape=(jax.ShapeDtypeStruct(shape, BF16),) * 2,
        in_specs=[pl.BlockSpec(memory_space=pltpu.SMEM)] + [pl.BlockSpec(memory_space=pl.ANY)] * 3,
        out_specs=(pl.BlockSpec(memory_space=pltpu.VMEM),) * 2,
        scratch_shapes=[pltpu.VMEM(shape, BF16)] * 6
        + [
            pltpu.VMEM((n * shard_rows, cols), BF16),
            pltpu.VMEM((cols, cols), F32),
            pltpu.VMEM((cols, cols), BF16),
            pltpu.VMEM((n * groups, 8, 128), F32),
            pltpu.SemaphoreType.DMA((3,)),
            pltpu.SemaphoreType.DMA((n * groups,)),
            pltpu.SemaphoreType.DMA((n * groups,)),
            pltpu.SemaphoreType.DMA((n,)),
            pltpu.SemaphoreType.DMA((n,)),
            pltpu.SemaphoreType.DMA((n,)),
            pltpu.SemaphoreType.DMA((n,)),
        ],
        compiler_params=pltpu.CompilerParams(
            collective_id=0, has_side_effects=True, vmem_limit_bytes=48 << 20
        ),
        name="muon_step",
    )(assign, weight[0], momentum[0], gradient[0])
    return new_weight[None], new_momentum[None]


def solution(mesh):
    placed = P("experts", None, "rows", None)
    return jax.shard_map(
        local,
        mesh=mesh,
        in_specs=(placed, placed, placed, P("experts", None)),
        out_specs=(placed, placed),
        check_vma=False,
    )
```

time: 77.3 us -> 75.6 us (0.978)
  the two profiles are of different devices: /device:TPU:1 before, /device:TPU:0 now
where the time goes in v2:
time: 75.6 us; the launch traced here: 75.5 us
  Pallas kernels  71.5 us (95%)
  local copies, waits for them, and re-layouts  3.29 us (4%)
    pallas_call x1, Pallas kernels, local(): pl.pallas_call(functools.partial(kernel, n, groups, block_rows), out_shap...  71.5 us
    unnamed x4, local copies, waits for them, and re-layouts  3.29 us

profile of v2, /device:TPU:0, one launch (start us, length us, event | category | flops | bytes accessed | tf_op | source)
XLA Modules:
  0.0 75.5 jit_solution(5869741155634096187)
XLA Ops:
  0.6 0.0 copy-start
  0.6 0.6 copy-done
  1.3 71.5 %muon_step.1 = (bf16[8,256,512]{2,1,0:T(8,128)(2,1)S(1)}, bf16[8,256,512]{2,1,0:T(8,128)(2,1)S(1)}) custom-call(s32[1,8]{1,0:T(1,128)S(1)} %copy-done, bf16[8,256,512]{2,1,0:T(8,128)(2,1)} %bitcast.7, bf16[8,256,512]{2,1,0:T(8,128)(2,1)} %bitcast.8, bf16[8,256,512]{2,1,0:T(8,128)(2,1)} %bitcast.9), custom_call_target="tpu_custom_call" | custom-call | tf_op jit(solution)/shard_map/muon_step/pallas_call | solution.py:251
  72.8 1.3 %copy.8 = bf16[1,8,256,512]{3,2,1,0:T(8,128)(2,1)} copy(bf16[1,8,256,512]{3,2,1,0:T(8,128)(2,1)S(1)} %bitcast.6) | data formatting | bytes 4194304
  74.2 1.3 %copy.9 = bf16[1,8,256,512]{3,2,1,0:T(8,128)(2,1)} copy(bf16[1,8,256,512]{3,2,1,0:T(8,128)(2,1)S(1)} %bitcast.5) | data formatting | bytes 4194304
Async XLA Ops:
  0.6 0.7 copy-start

commit v3 on v2

--- a/solution.py
+++ b/solution.py
@@ -55,8 +55,8 @@
     n, groups, block_rows,
     assign, w_hbm, m_hbm, g_hbm,
     nw_ref, nm_ref,
-    w_v, m_v, g_v, send_v, recv_v, back_v, x_v, gram_v, poly_v, part,
-    load_sem, s_send, s_recv, f_send, f_recv, b_send, b_recv,
+    w_v, m_v, g_v, send_v, recv_v, gram_v, poly_v, first_v, part, pack,
+    load_sem, s_send, s_recv, f_send, f_recv, p_send, p_recv,
 ):
     me = lax.axis_index("rows")
     group = lax.axis_index("experts")
@@ -151,6 +151,7 @@
     lax.fori_loop(1, n, send_update, 0)
     own = update_of(me)
     recv_v[me] = own
+    send_v[me] = own
     gram_v[...] = gram_of(own)
 
     def momentum_of(p, carry):
@@ -179,13 +180,12 @@
     trace = jnp.sum(jnp.where(diagonal, gram, 0.0), axis=(0, 1), keepdims=True)
     scale = 1.0 / (jnp.sqrt(trace) + norm_epsilon)
     gram_v[...] = gram * (scale * scale)
-    chain(first_steps, True, gram_v, poly_v)
+    chain(first_steps, True, gram_v, first_v)
 
     shards = block_rows // shard_rows
     for b in range(n // shards):
         x = recv_v[pl.ds(b * shards, shards)].reshape(block_rows, cols)
-        x = (scale * dot(x, poly_v[...])).astype(BF16)
-        x_v[pl.ds(b * block_rows, block_rows)] = x
+        x = (scale * dot(x, first_v[...])).astype(BF16)
         if b == 0:
             gram_v[...] = gram_of(x)
         else:
@@ -193,59 +193,113 @@
 
     chain(ITERS - first_steps, False, gram_v, poly_v)
 
-    def last_rows(i):
-        x = x_v[pl.ds(pl.multiple_of(i * shard_rows, shard_rows), shard_rows)]
-        return dot(x, poly_v[...]).astype(BF16)
-
-    def back_copy(target, source):
-        return pltpu.make_async_remote_copy(
-            src_ref=send_v.at[target],
-            dst_ref=back_v.at[source],
-            send_sem=b_send.at[target],
-            recv_sem=b_recv.at[source],
+    whole = (scale * dot(first_v[...], poly_v[...])).astype(BF16)
+    half = cols // 2
+    piece = half // 2
+    for q in range(2):
+        top = slice(q * piece, (q + 1) * piece)
+        bottom = slice(half + q * piece, half + (q + 1) * piece)
+        pack[me, q, 0] = whole[top, :half]
+        pack[me, q, 1] = whole[top, half:]
+        pack[me, q, 2] = whole[bottom, half:]
+
+    bits = (n // 2).bit_length() - 1
+    orders = (tuple(range(bits)), tuple(reversed(range(bits))))
+
+    def flip(index, bit):
+        return index + bit * (1 - 2 * lax.rem(lax.div(index, bit), 2))
+
+    def owner_of(mask):
+        index = me
+        for b in range(bits):
+            if mask >> b & 1:
+                index = flip(index, 2 << b)
+        return index
+
+    def onward(mask, q):
+        last = max((orders[q].index(b) for b in range(bits) if mask >> b & 1), default=-1)
+        return orders[q][last + 1 :]
+
+    sent = []
+
+    def send_piece(owner, q, target):
+        copy = pltpu.make_async_remote_copy(
+            src_ref=pack.at[owner, q],
+            dst_ref=pack.at[owner, q],
+            send_sem=p_send.at[len(sent)],
+            recv_sem=p_recv.at[owner, q],
             device_id={"rows": target},
             device_id_type=MESH,
         )
-
-    def send_back(k, carry):
-        target = peer(k)
-        forward_copy(target, me).wait_send()
-        send_v[target] = last_rows(target)
-        back_copy(target, me).start()
-        return carry
-
-    lax.fori_loop(1, n, send_back, 0)
+        copy.start()
+        sent.append(copy)
+
+    def wait_piece(owner, q):
+        pltpu.make_async_remote_copy(
+            src_ref=pack.at[owner, q],
+            dst_ref=pack.at[owner, q],
+            send_sem=p_send.at[0],
+            recv_sem=p_recv.at[owner, q],
+            device_id={"rows": flip(me, 1)},
+            device_id_type=MESH,
+        ).wait_recv()
+
     step = learn_rate * 0.2 * math.sqrt(max(n * shard_rows, cols))
+
+    def weight_of(i):
+        left = send_v[i, :, :half]
+        right = send_v[i, :, half:]
+        first, cross, second = (
+            jnp.concatenate([pack[i, 0, b], pack[i, 1, b]], axis=0) for b in range(3)
+        )
+        mirrored = lax.dot_general(right, cross, (((1,), (1,)), ((), ())), preferred_element_type=F32)
+        decay = 1.0 - learn_rate * weight_decay
+        nw_ref[i, :, :half] = (
+            w_v[i, :, :half].astype(F32) * decay - step * (dot(left, first) + mirrored)
+        ).astype(BF16)
+        nw_ref[i, :, half:] = (
+            w_v[i, :, half:].astype(F32) * decay - step * (dot(left, cross) + dot(right, second))
+        ).astype(BF16)
+
+    for level in range(bits):
+        for q in range(2):
+            send_piece(me, q, flip(me, 2 << orders[q][level]))
+    for q in range(2):
+        send_piece(me, q, flip(me, 1))
     load_w.wait()
-
-    def weight_of(i, ortho):
-        nw_ref[i] = (
-            w_v[i].astype(F32) * (1.0 - learn_rate * weight_decay) - step * ortho.astype(F32)
-        ).astype(BF16)
-
-    weight_of(me, last_rows(me))
-
-    def take_back(k, carry):
-        source = lax.rem(me + n - 1 - lax.rem(k, n - 1), n)
-        back_copy(source, source).wait_recv()
-        weight_of(source, back_v[source])
-        return carry
-
-    lax.fori_loop(1, n, take_back, 0)
+    weight_of(me)
+    masks = [[m for m in range(n // 2) if bin(m).count("1") == level] for level in range(bits + 1)]
+    for level in range(bits + 1):
+        if level > 0:
+            pieces = [(m, q) for m in masks[level] for q in range(2)]
+            for m, q in sorted(pieces, key=lambda at: -len(onward(*at))):
+                wait_piece(owner_of(m), q)
+                for b in onward(m, q):
+                    send_piece(owner_of(m), q, flip(me, 2 << b))
+                send_piece(owner_of(m), q, flip(me, 1))
+            for m in masks[level]:
+                weight_of(owner_of(m))
+        for m in masks[level]:
+            owner = flip(owner_of(m), 1)
+            for q in range(2):
+                wait_piece(owner, q)
+            weight_of(owner)
+
+    def drain_forward(k, carry):
+        forward_copy(peer(k), me).wait_send()
+        return carry
+
+    lax.fori_loop(1, n, drain_forward, 0)
     lax.fori_loop(1, devices, drain_sum, 0)
-
-    def drain_back(k, carry):
-        back_copy(lax.rem(me + k, n), me).wait_send()
-        return carry
-
-    lax.fori_loop(1, n, drain_back, 0)
+    for copy in sent:
+        copy.wait_send()
 
 
 def local(weight, momentum, gradient, assign):
     n = lax.axis_size("rows")
     groups = lax.axis_size("experts")
     _, slots, shard_rows, cols = gradient.shape
-    assert slots == n
+    assert slots == n and n & (n - 1) == 0
     block_rows = min(1024, n * shard_rows)
     shape = (slots, shard_rows, cols)
     new_weight, new_momentum = pl.pallas_call(
@@ -253,19 +307,20 @@
         out_shape=(jax.ShapeDtypeStruct(shape, BF16),) * 2,
         in_specs=[pl.BlockSpec(memory_space=pltpu.SMEM)] + [pl.BlockSpec(memory_space=pl.ANY)] * 3,
         out_specs=(pl.BlockSpec(memory_space=pltpu.VMEM),) * 2,
-        scratch_shapes=[pltpu.VMEM(shape, BF16)] * 6
+        scratch_shapes=[pltpu.VMEM(shape, BF16)] * 5
         + [
-            pltpu.VMEM((n * shard_rows, cols), BF16),
             pltpu.VMEM((cols, cols), F32),
             pltpu.VMEM((cols, cols), BF16),
+            pltpu.VMEM((cols, cols), BF16),
             pltpu.VMEM((n * groups, 8, 128), F32),
+            pltpu.VMEM((n, 2, 3, cols // 4, cols // 2), BF16),
             pltpu.SemaphoreType.DMA((3,)),
             pltpu.SemaphoreType.DMA((n * groups,)),
             pltpu.SemaphoreType.DMA((n * groups,)),
             pltpu.SemaphoreType.DMA((n,)),
             pltpu.SemaphoreType.DMA((n,)),
-            pltpu.SemaphoreType.DMA((n,)),
-            pltpu.SemaphoreType.DMA((n,)),
+            pltpu.SemaphoreType.DMA((2 * n,)),
+            pltpu.SemaphoreType.DMA((n, 2)),
         ],
         compiler_params=pltpu.CompilerParams(
             collective_id=0, has_side_effects=True, vmem_limit_bytes=48 << 20

time: 75.6 us -> 67.1 us (0.89)
  Pallas kernels: 71.5 us -> 63 us
    pallas_call x1, Pallas kernels: 71.5 us -> 63 us  [local(): pl.pallas_call(functools.partial(kernel, n, groups, block_rows), out_shap...]
where the time goes in v3:
time: 67.1 us; the launch traced here: 66.9 us
  Pallas kernels  63 us (94%)
  local copies, waits for them, and re-layouts  3.29 us (5%)
    pallas_call x1, Pallas kernels, local(): pl.pallas_call(functools.partial(kernel, n, groups, block_rows), out_shap...  63 us
    unnamed x4, local copies, waits for them, and re-layouts  3.29 us

profile of v3, /device:TPU:0, one launch (start us, length us, event | category | flops | bytes accessed | tf_op | source)
XLA Modules:
  0.0 66.9 jit_solution(8540211806333297686)
XLA Ops:
  0.6 0.0 copy-start
  0.6 0.6 copy-done
  1.3 63.0 %muon_step.1 = (bf16[8,256,512]{2,1,0:T(8,128)(2,1)S(1)}, bf16[8,256,512]{2,1,0:T(8,128)(2,1)S(1)}) custom-call(s32[1,8]{1,0:T(1,128)S(1)} %copy-done, bf16[8,256,512]{2,1,0:T(8,128)(2,1)} %bitcast.7, bf16[8,256,512]{2,1,0:T(8,128)(2,1)} %bitcast.8, bf16[8,256,512]{2,1,0:T(8,128)(2,1)} %bitcast.9), custom_call_target="tpu_custom_call" | custom-call | tf_op jit(solution)/shard_map/muon_step/pallas_call | solution.py:305
  64.3 1.3 %copy.8 = bf16[1,8,256,512]{3,2,1,0:T(8,128)(2,1)} copy(bf16[1,8,256,512]{3,2,1,0:T(8,128)(2,1)S(1)} %bitcast.6) | data formatting | bytes 4194304
  65.6 1.3 %copy.9 = bf16[1,8,256,512]{3,2,1,0:T(8,128)(2,1)} copy(bf16[1,8,256,512]{3,2,1,0:T(8,128)(2,1)S(1)} %bitcast.5) | data formatting | bytes 4194304
Async XLA Ops:
  0.6 0.7 copy-start

commit v4 on v3

--- a/solution.py
+++ b/solution.py
@@ -10,6 +10,7 @@
 
 ITERS = 5
 first_steps = 3
+tiles = 4
 linear_coef = 3.4445
 cubic_coef = -4.775
 quintic_coef = 2.0315
@@ -53,10 +54,10 @@
 
 def kernel(
     n, groups, block_rows,
-    assign, w_hbm, m_hbm, g_hbm,
+    assign_hbm, w_hbm, m_hbm, g_hbm,
     nw_ref, nm_ref,
-    w_v, m_v, g_v, send_v, recv_v, gram_v, poly_v, first_v, part, pack,
-    load_sem, s_send, s_recv, f_send, f_recv, p_send, p_recv,
+    w_v, m_v, g_v, send_v, recv_v, gram_v, poly_v, first_v, part, pack, full_v, assign,
+    load_sem, g_sem, s_send, s_recv, f_send, f_recv, p_send, p_recv,
 ):
     me = lax.axis_index("rows")
     group = lax.axis_index("experts")
@@ -76,15 +77,24 @@
         return carry
 
     lax.fori_loop(1, devices, greet, 0)
-    load_g = pltpu.make_async_copy(g_hbm, g_v, load_sem.at[0])
+
+    def load_g(i):
+        return pltpu.make_async_copy(g_hbm.at[i], g_v.at[i], g_sem.at[i])
+
+    def start_g(i, carry):
+        load_g(i).start()
+        return carry
+
+    lax.fori_loop(0, slots, start_g, 0)
+    load_a = pltpu.make_async_copy(assign_hbm, assign, load_sem.at[0])
     load_m = pltpu.make_async_copy(m_hbm, m_v, load_sem.at[1])
     load_w = pltpu.make_async_copy(w_hbm, w_v, load_sem.at[2])
-    load_g.start()
+    load_a.start()
     load_m.start()
     load_w.start()
-    load_g.wait()
 
     def square_sum(i, total):
+        load_g(i).wait()
         wide = g_v[i].astype(F32)
         return total + jnp.sum((wide * wide).reshape(shard_rows // 8, 8, cols), axis=0)
 
@@ -119,6 +129,7 @@
 
     lax.fori_loop(1, devices, start_sum, 0)
     load_m.wait()
+    load_a.wait()
     lax.fori_loop(1, devices, wait_sum, 0)
     sum_squares = jnp.sum(jnp.sum(part[...], axis=0), axis=(0, 1), keepdims=True)
     clip_limit = math.sqrt(float(slots * shard_rows * cols * n * groups))
@@ -194,14 +205,15 @@
     chain(ITERS - first_steps, False, gram_v, poly_v)
 
     whole = (scale * dot(first_v[...], poly_v[...])).astype(BF16)
-    half = cols // 2
-    piece = half // 2
-    for q in range(2):
-        top = slice(q * piece, (q + 1) * piece)
-        bottom = slice(half + q * piece, half + (q + 1) * piece)
-        pack[me, q, 0] = whole[top, :half]
-        pack[me, q, 1] = whole[top, half:]
-        pack[me, q, 2] = whole[bottom, half:]
+    side = cols // tiles
+    places = [(r, c) for r in range(tiles) for c in range(r, tiles)]
+    half = len(places) // 2
+
+    def cut(r):
+        return slice(r * side, (r + 1) * side)
+
+    for at, (r, c) in enumerate(places):
+        pack[me, at // half, at % half] = whole[cut(r), cut(c)]
 
     bits = (n // 2).bit_length() - 1
     orders = (tuple(range(bits)), tuple(reversed(range(bits))))
@@ -247,18 +259,14 @@
     step = learn_rate * 0.2 * math.sqrt(max(n * shard_rows, cols))
 
     def weight_of(i):
-        left = send_v[i, :, :half]
-        right = send_v[i, :, half:]
-        first, cross, second = (
-            jnp.concatenate([pack[i, 0, b], pack[i, 1, b]], axis=0) for b in range(3)
-        )
-        mirrored = lax.dot_general(right, cross, (((1,), (1,)), ((), ())), preferred_element_type=F32)
+        for at, (r, c) in enumerate(places):
+            tile = pack[i, at // half, at % half]
+            full_v[cut(r), cut(c)] = tile
+            if r != c:
+                full_v[cut(c), cut(r)] = tile.T
         decay = 1.0 - learn_rate * weight_decay
-        nw_ref[i, :, :half] = (
-            w_v[i, :, :half].astype(F32) * decay - step * (dot(left, first) + mirrored)
-        ).astype(BF16)
-        nw_ref[i, :, half:] = (
-            w_v[i, :, half:].astype(F32) * decay - step * (dot(left, cross) + dot(right, second))
+        nw_ref[i] = (
+            w_v[i].astype(F32) * decay - step * dot(send_v[i], full_v[...])
         ).astype(BF16)
 
     for level in range(bits):
@@ -305,7 +313,7 @@
     new_weight, new_momentum = pl.pallas_call(
         functools.partial(kernel, n, groups, block_rows),
         out_shape=(jax.ShapeDtypeStruct(shape, BF16),) * 2,
-        in_specs=[pl.BlockSpec(memory_space=pltpu.SMEM)] + [pl.BlockSpec(memory_space=pl.ANY)] * 3,
+        in_specs=[pl.BlockSpec(memory_space=pltpu.HBM)] * 4,
         out_specs=(pl.BlockSpec(memory_space=pltpu.VMEM),) * 2,
         scratch_shapes=[pltpu.VMEM(shape, BF16)] * 5
         + [
@@ -313,8 +321,11 @@
             pltpu.VMEM((cols, cols), BF16),
             pltpu.VMEM((cols, cols), BF16),
             pltpu.VMEM((n * groups, 8, 128), F32),
-            pltpu.VMEM((n, 2, 3, cols // 4, cols // 2), BF16),
+            pltpu.VMEM((n, 2, tiles * (tiles + 1) // 4, cols // tiles, cols // tiles), BF16),
+            pltpu.VMEM((cols, cols), BF16),
+            pltpu.SMEM((1, slots), jnp.int32),
             pltpu.SemaphoreType.DMA((3,)),
+            pltpu.SemaphoreType.DMA((n,)),
             pltpu.SemaphoreType.DMA((n * groups,)),
             pltpu.SemaphoreType.DMA((n * groups,)),
             pltpu.SemaphoreType.DMA((n,)),

time: 67.1 us -> 64.1 us (0.955)
  Pallas kernels: 63 us -> 60 us
    pallas_call x1, Pallas kernels: 63 us -> 60 us  [local(): pl.pallas_call(functools.partial(kernel, n, groups, block_rows), out_shap...]
where the time goes in v4:
time: 64.1 us; the launch traced here: 64 us
  Pallas kernels  60 us (94%)
  local copies, waits for them, and re-layouts  3.29 us (5%)
  between operations  0.65 us (1%)
    pallas_call x1, Pallas kernels, local(): pl.pallas_call(functools.partial(kernel, n, groups, block_rows), out_shap...  60 us
    unnamed x4, local copies, waits for them, and re-layouts  3.29 us

profile of v4, /device:TPU:0, one launch (start us, length us, event | category | flops | bytes accessed | tf_op | source)
XLA Modules:
  0.0 64.0 jit_solution(5987700470024983050)
XLA Ops:
  0.6 0.0 copy-start
  0.6 0.6 %copy-done = s32[1,8]{1,0:T(1,128)S(1)} copy-done((s32[1,8]{1,0:T(1,128)S(1)}, s32[1,8]{1,0:T(1,128)}, u32[]{:S(2)}) %copy-start) | copy-done | bytes 56
  1.3 60.0 %muon_step.1 = (bf16[8,256,512]{2,1,0:T(8,128)(2,1)S(1)}, bf16[8,256,512]{2,1,0:T(8,128)(2,1)S(1)}) custom-call(s32[1,8]{1,0:T(1,128)S(1)} %copy-done, bf16[8,256,512]{2,1,0:T(8,128)(2,1)} %bitcast.7, bf16[8,256,512]{2,1,0:T(8,128)(2,1)} %bitcast.8, bf16[8,256,512]{2,1,0:T(8,128)(2,1)} %bitcast.9), custom_call_target="tpu_custom_call" | custom-call | tf_op jit(solution)/shard_map/muon_step/pallas_call | solution.py:313
  61.3 1.3 %copy.8 = bf16[1,8,256,512]{3,2,1,0:T(8,128)(2,1)} copy(bf16[1,8,256,512]{3,2,1,0:T(8,128)(2,1)S(1)} %bitcast.6) | data formatting | bytes 4194304
  62.6 1.3 %copy.9 = bf16[1,8,256,512]{3,2,1,0:T(8,128)(2,1)} copy(bf16[1,8,256,512]{3,2,1,0:T(8,128)(2,1)S(1)} %bitcast.5) | data formatting | bytes 4194304
Async XLA Ops:
  0.6 0.7 %copy-start = (s32[1,8]{1,0:T(1,128)S(1)}, s32[1,8]{1,0:T(1,128)}, u32[]{:S(2)}) copy-start(s32[1,8]{1,0:T(1,128)} %assign_hbm.1) | copy-start | bytes 100
